TPU v7x, 512 devices: a whole 4x8x8 slice. The times are simulated.
512 devices in a mesh: req: 128 (over z, y, core), rep: 4 (over x).
Axes of the slice: x: 4, y: 8, z: 8, core: 2. Of those that a mesh axis runs over, the one named last changes fastest.
Arguments:
- prefill_qkv: bfloat16 [65536, 3, 1792], P(('rep', 'req')), parts along dimension 0, may hold values from -6 to 6
- decode_qkv: bfloat16 [4096, 3, 1792], P(('rep', 'req')), parts along dimension 0, may hold values from -6 to 6
- conv_state: bfloat16 [4608, 2, 1792], P(('rep', 'req')), parts along dimension 0, may hold values from -6 to 6
- cache_len: int32 [4608], P(('rep', 'req')), parts along dimension 0, may hold values from 0 to 32768, as said below
- page_table: int32 [4608, 256], P(('rep', 'req')), parts along dimension 0, may hold values from 0 to 1
- page_pool: bfloat16 [1024, 2, 128, 1792], P(('rep', 'req')), parts along dimension 0, may hold values from -6 to 6
- conv_taps: float32 [3, 1792], replicated, may hold values from -3.5 to 3.5
- segment_owner: int32 [512], P('rep'), parts along dimension 0, may hold values from 0 to 127, each once
- regroup: int32 [69632], P('rep'), parts along dimension 0, may hold values from 0 to 17407, as said below
- residual: bfloat16 [69632, 1792], P(('rep', 'req')), parts along dimension 0, may hold values from -4 to 4
- norm_gain: float32 [1792], replicated, may hold values from 0.5 to 1.5
Outputs:
- new_residual: bfloat16 [69632, 1792], P(('rep', 'req')), parts along dimension 0
- normed: bfloat16 [69632, 1792], P(('rep', 'req')), parts along dimension 0
There are 4 independent parts, one for each index of `rep`. A program takes and returns all parts, laid end to end along the dimension named above; an argument that names none is the same for every part. Nothing has to cross between parts.
Inputs may be any that keep to these rules, and one draw needn't show every extreme that they name: `cache_len`: some request holds exactly 32768 cached positions. `page_table`: page numbers index the serving device's own 2 pages. `segment_owner`: A permutation of the devices: every device serves exactly one segment. `regroup`: A permutation: live row g goes to device (g + R) mod 128 for one drawn R, so every device receives 136 rows, and at most 2 rows go from one device to one device, a bound that every device reaches.
All inputs are finite; a program needn't handle non-finite values.
Results may differ from a plain program's by a relative error of at most 0.0052.
Values may be sent and summed in bfloat16 or wider, within the bound.
A program may use at most 128 MiB of HBM per device.

v0:
```python
import functools

import jax
import jax.numpy as jnp
from jax import lax
from jax.experimental import pallas as pl
from jax.experimental.pallas import tpu as pltpu
from jax.sharding import PartitionSpec as P

HEADS = 16
HEAD_CHANNELS = 112
WINDOW = 64
PAGE = 128
LANES = 128

norm_eps = 1e-06
masked_score = -1e30
F32 = jnp.float32
BF16 = jnp.bfloat16
I32 = jnp.int32


def iota(shape, dim):
    return lax.broadcasted_iota(I32, shape, dim)


def dot_nt(a, b):
    return lax.dot_general(a, b, (((1,), (1,)), ((), ())), preferred_element_type=F32)


def rotation(regroup_ref, even_rows, devices):
    first = regroup_ref[0:1, 0:1]
    starts = iota((1, devices), 1) * even_rows
    return jnp.sum((starts <= first).astype(I32), axis=1, keepdims=True) - 1


def attention_kernel(
    devices,
    even_rows,
    cache_len_ref,
    page_table_ref,
    q_ref,
    k_ref,
    v_ref,
    tail_ref,
    dq_ref,
    dk_ref,
    dv_ref,
    dt0_ref,
    dt1_ref,
    pool_ref,
    taps_ref,
    regroup_ref,
    out_ref,
    extended,
    keys,
    values,
    context,
    dec_queries,
    dec_scores,
):
    me = lax.axis_index("req")
    rows = q_ref.shape[0]
    width = q_ref.shape[1]
    decodes = dq_ref.shape[0]
    scale = HEAD_CHANNELS ** (-0.5)

    def window_pages(r):
        cached = cache_len_ref[r]
        top = jnp.maximum((cached - 1) >> 7, 0)
        below = jnp.maximum(top - 1, 0)
        return cached, top, page_table_ref[r, top], page_table_ref[r, below]

    def cached_positions(r, shape, dim):
        cached, top, at_top, at_below = window_pages(r)
        offset = iota(shape, dim)
        position = cached - 1 - ((cached - 1 - offset) & (PAGE - 1))
        page = jnp.where(position >= top * PAGE, at_top, at_below)
        return cached, position, page

    _, _, page = cached_positions(0, (PAGE, width), 0)
    first_page = page == 0
    keys[0:PAGE, :] = jnp.where(
        first_page, pool_ref[0, 0].astype(F32), pool_ref[1, 0].astype(F32)
    ).astype(BF16)
    values[0:PAGE, :] = jnp.where(
        first_page, pool_ref[0, 1].astype(F32), pool_ref[1, 1].astype(F32)
    ).astype(BF16)
    extended[6:8, :] = tail_ref[...].astype(F32)
    extended[8 : 8 + rows, :] = k_ref[...].astype(F32)
    keys[PAGE : PAGE + rows, :] = (
        taps_ref[0:1, :] * extended[6 : 6 + rows, :]
        + taps_ref[1:2, :] * extended[7 : 7 + rows, :]
        + taps_ref[2:3, :] * extended[8 : 8 + rows, :]
    ).astype(BF16)
    values[PAGE : PAGE + rows, :] = v_ref[...]

    cached, position, _ = cached_positions(0, (rows, PAGE), 1)
    token = iota((rows, PAGE), 0)
    ok_cached = (position >= 0) & (position >= cached + token - (WINDOW - 1))
    other = iota((rows, rows), 1)
    token = iota((rows, rows), 0)
    ok_fresh = (other <= token) & (other >= token - (WINDOW - 1))
    bias = jnp.concatenate(
        [
            jnp.where(ok_cached, 0.0, masked_score).astype(F32),
            jnp.where(ok_fresh, 0.0, masked_score).astype(F32),
        ],
        axis=1,
    )

    context[...] = jnp.zeros_like(context)
    for head in range(HEADS):
        low, high = head * HEAD_CHANNELS, (head + 1) * HEAD_CHANNELS
        start = low // LANES * LANES
        stop = -(-high // LANES) * LANES
        lane = iota((rows, stop - start), 1) + start
        mine = (lane >= low) & (lane < high)
        query = jnp.where(mine, q_ref[:, start:stop].astype(F32), 0.0).astype(BF16)
        scores = dot_nt(query, keys[:, start:stop]) * scale + bias
        top = jnp.max(scores, axis=1, keepdims=True)
        raised = jnp.exp(scores - top)
        weights = (raised * (1.0 / jnp.sum(raised, axis=1, keepdims=True))).astype(BF16)
        part = jnp.dot(weights, values[:, start:stop], preferred_element_type=F32)
        context[:, start:stop] = jnp.where(mine, part, context[:, start:stop])

    lane = iota((HEADS, width), 1)
    low = iota((HEADS, width), 0) * HEAD_CHANNELS
    mine = (lane >= low) & (lane < low + HEAD_CHANNELS)
    fresh = (
        taps_ref[0:1, :] * dt0_ref[...].astype(F32)
        + taps_ref[1:2, :] * dt1_ref[...].astype(F32)
        + taps_ref[2:3, :] * dk_ref[...].astype(F32)
    ).astype(BF16).astype(F32)
    queries = dq_ref[...].astype(F32)
    new_values = dv_ref[...].astype(F32)
    own = []
    bias_rows = []
    for r in range(decodes):
        spread = jnp.where(mine, queries[r : r + 1, :], 0.0)
        dec_queries[r * HEADS : (r + 1) * HEADS, :] = spread.astype(BF16)
        own.append(jnp.sum(spread * fresh[r : r + 1, :], axis=1, keepdims=True))
        cached, position, page = cached_positions(1 + r, (HEADS, PAGE), 1)
        ok = (position >= 0) & (position >= cached - (WINDOW - 1))
        bias_rows.append(
            jnp.concatenate(
                [
                    jnp.where(ok & (page == n), 0.0, masked_score).astype(F32)
                    for n in range(2)
                ],
                axis=1,
            )
        )
    own = jnp.concatenate(own, axis=0) * scale
    scores = jnp.concatenate(
        [dot_nt(dec_queries[...], pool_ref[n, 0]) for n in range(2)], axis=1
    )
    scores = scores * scale + jnp.concatenate(bias_rows, axis=0)
    top = jnp.maximum(jnp.max(scores, axis=1, keepdims=True), own)
    raised = jnp.exp(scores - top)
    own = jnp.exp(own - top)
    total = 1.0 / (jnp.sum(raised, axis=1, keepdims=True) + own)
    weights = (raised * total).astype(BF16)
    own = (own * total).astype(BF16).astype(F32)
    dec_scores[...] = jnp.dot(
        weights[:, :PAGE], pool_ref[0, 1], preferred_element_type=F32
    ) + jnp.dot(weights[:, PAGE:], pool_ref[1, 1], preferred_element_type=F32)
    dec_rows = []
    for r in range(decodes):
        span = slice(r * HEADS, (r + 1) * HEADS)
        mixed = dec_scores[span, :] + own[span, :] * new_values[r : r + 1, :]
        dec_rows.append(jnp.sum(jnp.where(mine, mixed, 0.0), axis=0, keepdims=True))
    dec_context = jnp.concatenate(dec_rows, axis=0).astype(BF16)

    turn = rotation(regroup_ref, even_rows, devices)
    target = iota((devices, rows), 0)
    chosen = ((target - turn) & (devices - 1)) == iota((devices, rows), 1)
    out_ref[:, :width] = jnp.dot(
        chosen.astype(F32).astype(BF16),
        context[...].astype(BF16),
        preferred_element_type=F32,
    ).astype(BF16)
    target = iota((devices, decodes), 0)
    number = me * decodes + iota((devices, decodes), 1)
    chosen = ((target - turn) & (devices - 1)) == (number & (devices - 1))
    out_ref[:, width:] = jnp.dot(
        chosen.astype(F32).astype(BF16), dec_context, preferred_element_type=F32
    ).astype(BF16)


def finish_kernel(
    devices, arrived_ref, residual_ref, gain_ref, regroup_ref, owner_ref, sum_ref, norm_ref
):
    me = lax.axis_index("req")
    even_rows, width = residual_ref.shape
    decodes = even_rows - devices
    token = (me - rotation(regroup_ref, even_rows, devices)) & (devices - 1)

    column = jnp.sum(
        jnp.where(iota((even_rows, devices), 1) == token, regroup_ref[...], 0),
        axis=1,
        keepdims=True,
    ) - me * even_rows

    def as_row(part):
        size = part.shape[0]
        diagonal = iota((size, devices), 0) == iota((size, devices), 1)
        return jnp.sum(jnp.where(diagonal, part, 0), axis=0, keepdims=True)

    lands = (iota((even_rows, devices), 0) == as_row(column[:devices])).astype(F32)
    diagonal = iota((devices, devices), 0) == iota((devices, devices), 1)
    owner = jnp.sum(jnp.where(diagonal, owner_ref[...], 0), axis=1, keepdims=True)
    came = (iota((devices, devices), 1) == owner).astype(F32)
    pick = jnp.dot(lands.astype(BF16), came.astype(BF16), preferred_element_type=F32)
    gathered = jnp.dot(
        pick.astype(BF16), arrived_ref[:, :width], preferred_element_type=F32
    )

    lane = iota((even_rows, devices), 1)
    lands = (iota((even_rows, devices), 0) == as_row(column[devices:])) & (lane < decodes)
    stride = devices // decodes
    source = (token >> (decodes.bit_length() - 1)) + iota((devices, devices), 0) * stride
    came = (iota((devices, devices), 1) == source).astype(F32)
    pick = jnp.dot(
        lands.astype(F32).astype(BF16), came.astype(BF16), preferred_element_type=F32
    )
    gathered += jnp.dot(
        pick.astype(BF16), arrived_ref[:, width:], preferred_element_type=F32
    )
    summed = residual_ref[...].astype(F32) + gathered
    inverse_rms = lax.rsqrt(jnp.mean(summed * summed, axis=1, keepdims=True) + norm_eps)
    sum_ref[...] = summed.astype(BF16)
    norm_ref[...] = (summed * inverse_rms * gain_ref[...]).astype(BF16)


def body(
    prefill_qkv,
    decode_qkv,
    conv_state,
    cache_len,
    page_table,
    page_pool,
    conv_taps,
    segment_owner,
    regroup,
    residual,
    norm_gain,
):
    devices = lax.axis_size("req")
    rows, _, width = prefill_qkv.shape
    decodes = decode_qkv.shape[0]
    even_rows = residual.shape[0]
    table = regroup.reshape(regroup.shape[0] // devices, devices)
    owner = segment_owner.reshape(1, devices)
    smem = pl.BlockSpec(memory_space=pltpu.SMEM)
    vmem = pl.BlockSpec(memory_space=pltpu.VMEM)
    packed = pl.pallas_call(
        functools.partial(attention_kernel, devices, even_rows),
        out_shape=jax.ShapeDtypeStruct((devices, 2 * width), BF16),
        in_specs=[smem, smem] + [vmem] * 12,
        out_specs=vmem,
        scratch_shapes=[
            pltpu.VMEM((rows + 8, width), F32),
            pltpu.VMEM((PAGE + rows, width), BF16),
            pltpu.VMEM((PAGE + rows, width), BF16),
            pltpu.VMEM((rows, width), F32),
            pltpu.VMEM((decodes * HEADS, width), BF16),
            pltpu.VMEM((decodes * HEADS, width), F32),
        ],
        name="attention",
    )(
        cache_len,
        page_table,
        prefill_qkv[:, 0],
        prefill_qkv[:, 1],
        prefill_qkv[:, 2],
        conv_state[0],
        decode_qkv[:, 0],
        decode_qkv[:, 1],
        decode_qkv[:, 2],
        conv_state[1:, 0],
        conv_state[1:, 1],
        page_pool,
        conv_taps,
        table,
    )
    arrived = lax.all_to_all(packed, "req", split_axis=0, concat_axis=0, tiled=True)
    out = jax.ShapeDtypeStruct((even_rows, width), BF16)
    return pl.pallas_call(
        functools.partial(finish_kernel, devices),
        out_shape=(out, out),
        in_specs=[vmem] * 5,
        out_specs=(vmem, vmem),
        name="finish",
    )(arrived, residual, norm_gain.reshape(1, width), table, owner)


def solution(mesh):
    in_specs = (
        P(("rep", "req"), None, None),
        P(("rep", "req"), None, None),
        P(("rep", "req"), None, None),
        P(("rep", "req")),
        P(("rep", "req"), None),
        P(("rep", "req"), None, None, None),
        P(),
        P("rep"),
        P("rep"),
        P(("rep", "req"), None),
        P(),
    )
    out_specs = (P(("rep", "req"), None), P(("rep", "req"), None))
    return jax.shard_map(body, mesh=mesh, in_specs=in_specs, out_specs=out_specs, check_vma=False)
```

profile of v0, /device:TPU:1, one launch (start us, length us, event | category | flops | bytes accessed | tf_op | source)
XLA Modules:
  0.0 72.5 jit_solution(13696189133422506787)
XLA Ops:
  0.6 0.0 copy-start
  0.6 1.0 %fusion = (bf16[8,1,1792]{2,1,0:T(2,128)(2,1)S(1)}, bf16[8,1,1792]{2,1,0:T(2,128)(2,1)S(1)}) fusion(bf16[9,2,1792]{2,1,0:T(2,128)(2,1)} %param.13), kind=kLoop, calls=%fused_computation.10 | loop fusion | bytes 114688 | tf_op jit(solution)/shard_map/slice | solution.py:282
  1.6 1.3 %slice_bitcast_fusion.6.tail_ref = bf16[2,1792]{1,0:T(2,128)(2,1)} fusion(bf16[9,2,1792]{2,1,0:T(2,128)(2,1)} %param.13), kind=kLoop, calls=%fused_computation.9 | loop fusion | bytes 14336 | tf_op jit(solution)/shard_map/squeeze | solution.py:277
  2.9 2.4 %slice_bitcast_fusion = (bf16[128,1792]{1,0:T(8,128)(2,1)}, bf16[128,1792]{1,0:T(8,128)(2,1)}, bf16[128,1792]{1,0:T(8,128)(2,1)}) fusion(bf16[128,3,1792]{2,0,1:T(8,128)(2,1)} %param.11), kind=kLoop, calls=%fused_computation.1 | loop fusion | bytes 2752512 | tf_op jit(solution)/shard_map/squeeze | solution.py:276
  5.3 0.0 copy-done
  5.3 0.6 slice_bitcast_fusion.3
  6.0 0.6 copy_bitcast_fusion.1
  6.6 9.8 %attention.1 = bf16[128,3584]{1,0:T(8,128)(2,1)} custom-call(s32[9]{0:T(128)} %cache_len_ref.1, s32[9,256]{1,0:T(8,128)} %page_table_ref.1, bf16[128,1792]{1,0:T(8,128)(2,1)} %get-tuple-element.3.q_ref, bf16[128,1792]{1,0:T(8,128)(2,1)} %get-tuple-element.4.k_ref, bf16[128,1792]{1,0:T(8,128)(2,1)} %get-tuple-element.2.v_ref, ...), custom_call_target="tpu_custom_call" | custom-call | tf_op jit(solution)/shard_map/attention/pallas_call | solution.py:257
  16.4 0.5 broadcast
  16.9 2.5 %reduce = bf16[128,3584]{1,0:T(8,128)(2,1)S(1)} reduce(bf16[128,1,3584]{2,0,1:T(8,128)(2,1)} %bitcast.24, bf16[]{:T(256)} %broadcast), dimensions={1}, to_apply=%copy.20.reduce_sub_computation | reduce | bytes 1835010 | tf_op jit(solution)/shard_map/all_to_all | solution.py:287
  19.4 0.0 copy-start.1
  19.4 1.1 %reshape.18 = bf16[128,2,1792]{2,1,0:T(2,128)(2,1)} reshape(bf16[128,3584]{1,0:T(8,128)(2,1)S(1)} %reduce) | data formatting | bytes 1835008
  20.5 18.4 %all-to-all-start = ((bf16[128,2,1792]{2,1,0:T(2,128)(2,1)}), bf16[128,2,1792]{2,1,0:T(2,128)(2,1)S(1)}, u32[]{:S(2)}, u32[]{:S(2)}) async-start(bf16[128,2,1792]{2,1,0:T(2,128)(2,1)} %reshape.18), calls=%async_computation | async-start | bytes 1835008 | tf_op jit(solution)/shard_map/all_to_all | solution.py:287
  38.9 0.0 copy-done.1
  39.0 0.6 reshape.16.gain_ref
  39.6 28.0 %all-to-all-done = bf16[128,2,1792]{2,1,0:T(2,128)(2,1)S(1)} async-done(((bf16[128,2,1792]{2,1,0:T(2,128)(2,1)}), bf16[128,2,1792]{2,1,0:T(2,128)(2,1)S(1)}, u32[]{:S(2)}, u32[]{:S(2)}) %all-to-all-start) | async-done | bytes 917536 | tf_op jit(solution)/shard_map/all_to_all | solution.py:287
  67.5 0.7 reshape.19
  68.3 1.1 %copy.27 = bf16[128,1,3584]{2,0,1:T(8,128)(2,1)} copy(bf16[128,1,3584]{2,1,0:T(2,128)(2,1)S(1)} %reshape.19) | data formatting | bytes 1835008
  69.3 3.2 %finish.1 = (bf16[136,1792]{1,0:T(8,128)(2,1)}, bf16[136,1792]{1,0:T(8,128)(2,1)}) custom-call(bf16[128,3584]{1,0:T(8,128)(2,1)} %bitcast.25, bf16[136,1792]{1,0:T(8,128)(2,1)} %residual_ref.1, f32[1,1792]{1,0:T(1,128)} %reshape.16.gain_ref, s32[136,128]{1,0:T(8,128)} %bitcast.27, s32[1,128]{1,0:T(1,128)} %bitcast.28), custom_call_target="tpu_custom_call" | custom-call | tf_op jit(solution)/shard_map/finish/pallas_call | solution.py:289
Async XLA Ops:
  0.6 4.7 %copy-start = (bf16[8,3,1792]{2,0,1:T(8,128)(2,1)S(1)}, bf16[8,3,1792]{2,0,1:T(8,128)(2,1)}, u32[]{:S(2)}) copy-start(bf16[8,3,1792]{2,0,1:T(8,128)(2,1)} %param.12) | copy-start | bytes 258052
  19.4 19.6 %copy-start.1 = (f32[1792]{0:T(1024)S(1)}, f32[1792]{0:T(1024)}, u32[]{:S(2)}) copy-start(f32[1792]{0:T(1024)} %param.21) | copy-start | bytes 21508
  20.5 47.0 %all-to-all-start = ((bf16[128,2,1792]{2,1,0:T(2,128)(2,1)}), bf16[128,2,1792]{2,1,0:T(2,128)(2,1)S(1)}, u32[]{:S(2)}, u32[]{:S(2)}) async-start(bf16[128,2,1792]{2,1,0:T(2,128)(2,1)} %reshape.18), calls=%async_computation | async-start | bytes 1835008 | tf_op jit(solution)/shard_map/all_to_all | solution.py:287
where the time goes:
time: 72.9 us; the launch traced here: 72.5 us
  waiting for transfers between devices  28 us (38%)
  starting transfers between devices  18.4 us (25%)
  Pallas kernels  13 us (18%)
  local copies, waits for them, and re-layouts  10 us (14%)
  other arithmetic  2.48 us (3%)
    all_to_all x1, waiting for transfers between devices, body(): lax.all_to_all(packed, 'req', split_axis=0, concat_axis=0, tiled=True)  28 us
    all_to_all x1, starting transfers between devices, body(): lax.all_to_all(packed, 'req', split_axis=0, concat_axis=0, tiled=True)  18.4 us
    pallas_call x1, Pallas kernels, body(): pl.pallas_call(functools.partial(attention_kernel, devices, even_rows), o...  9.77 us
    pallas_call x1, Pallas kernels, body(): pl.pallas_call(functools.partial(finish_kernel, devices), out_shape=(out,...  3.18 us
    unnamed x7, local copies, waits for them, and re-layouts  2.94 us
    all_to_all x1, other arithmetic, body(): lax.all_to_all(packed, 'req', split_axis=0, concat_axis=0, tiled=True)  2.48 us
    squeeze x1, local copies, waits for them, and re-layouts, body(): prefill_qkv[:, 2]  2.4 us
  transfers between devices with their start and end apart: 1, of which 1 were waited for; matrix products, arithmetic and copies ran while one was open for 1% of the time, Pallas kernels for 0%

commit v1 on v0

v1 whole, which is shorter than its diff:
```python
import functools

import jax
import jax.numpy as jnp
from jax import lax
from jax.experimental import pallas as pl
from jax.experimental.pallas import tpu as pltpu
from jax.sharding import PartitionSpec as P

HEADS = 16
HEAD_CHANNELS = 112
WINDOW = 64
PAGE = 128
LANES = 128
STRIDE = 37
MESH = pl.DeviceIdType.MESH

norm_eps = 1e-06
masked_score = -1e30
F32 = jnp.float32
BF16 = jnp.bfloat16
I32 = jnp.int32


def iota(shape, dim):
    return lax.broadcasted_iota(I32, shape, dim)


def dot_nt(a, b):
    return lax.dot_general(a, b, (((1,), (1,)), ((), ())), preferred_element_type=F32)


def rotation(regroup_ref, even_rows, devices):
    first = regroup_ref[0:1, 0:1]
    starts = iota((1, devices), 1) * even_rows
    return jnp.sum((starts <= first).astype(I32), axis=1, keepdims=True) - 1


def exchange_kernel(
    devices,
    even_rows,
    cache_len_ref,
    page_table_ref,
    table_ref,
    qkv_ref,
    dqkv_ref,
    state_ref,
    pool_ref,
    taps_ref,
    arrived_ref,
    extended,
    keys,
    values,
    context,
    dec_queries,
    dec_scores,
    state,
    dec_context,
    wide,
    dec_wide,
    send,
    dec_rows,
    near_send,
    near_recv,
    far_send,
    send_sem,
    recv_sem,
    near_sems,
    far_sems,
    own_sems,
    head,
):
    me = lax.axis_index("req")
    rows = qkv_ref.shape[1]
    width = qkv_ref.shape[2]
    decodes = dqkv_ref.shape[1]
    chunks = width // LANES
    near = devices // decodes
    far = decodes
    place, plane = lax.rem(me, near), lax.div(me, near)
    scale = HEAD_CHANNELS ** (-0.5)
    first = pltpu.make_async_copy(
        table_ref.at[pl.ds(0, 8)], head, own_sems.at[0]
    )
    first.start()

    barrier = pltpu.get_barrier_semaphore()

    @pl.loop(1, devices)
    def _(step):
        peer = lax.rem(me + step, devices)
        pl.semaphore_signal(
            barrier, inc=1, device_id={"req": peer}, device_id_type=MESH
        )

    def cached_positions(r, shape, dim):
        cached = cache_len_ref[r]
        top = jnp.maximum((cached - 1) >> 7, 0)
        below = jnp.maximum(top - 1, 0)
        at_top, at_below = page_table_ref[r, top], page_table_ref[r, below]
        offset = iota(shape, dim)
        position = cached - 1 - ((cached - 1 - offset) & (PAGE - 1))
        page = jnp.where(position >= top * PAGE, at_top, at_below)
        return cached, position, page

    state[...] = state_ref[...].astype(F32)

    lane = iota((HEADS, width), 1)
    low = iota((HEADS, width), 0) * HEAD_CHANNELS
    mine = (lane >= low) & (lane < low + HEAD_CHANNELS)
    fresh = (
        taps_ref[0:1, :] * state[1 : 1 + decodes, 0, :]
        + taps_ref[1:2, :] * state[1 : 1 + decodes, 1, :]
        + taps_ref[2:3, :] * dqkv_ref[1].astype(F32)
    ).astype(BF16).astype(F32)
    queries = dqkv_ref[0].astype(F32)
    new_values = dqkv_ref[2].astype(F32)
    own = []
    bias_rows = []
    for r in range(decodes):
        spread = jnp.where(mine, queries[r : r + 1, :], 0.0)
        dec_queries[r * HEADS : (r + 1) * HEADS, :] = spread.astype(BF16)
        own.append(jnp.sum(spread * fresh[r : r + 1, :], axis=1, keepdims=True))
        cached, position, page = cached_positions(1 + r, (HEADS, PAGE), 1)
        ok = (position >= 0) & (position >= cached - (WINDOW - 1))
        bias_rows.append(
            jnp.concatenate(
                [
                    jnp.where(ok & (page == n), 0.0, masked_score).astype(F32)
                    for n in range(2)
                ],
                axis=1,
            )
        )
    own = jnp.concatenate(own, axis=0) * scale
    scores = jnp.concatenate(
        [dot_nt(dec_queries[...], pool_ref[n, 0]) for n in range(2)], axis=1
    )
    scores = scores * scale + jnp.concatenate(bias_rows, axis=0)
    top = jnp.maximum(jnp.max(scores, axis=1, keepdims=True), own)
    raised = jnp.exp(scores - top)
    own = jnp.exp(own - top)
    total = 1.0 / (jnp.sum(raised, axis=1, keepdims=True) + own)
    weights = (raised * total).astype(BF16)
    own = (own * total).astype(BF16).astype(F32)
    dec_scores[...] = jnp.dot(
        weights[:, :PAGE], pool_ref[0, 1], preferred_element_type=F32
    ) + jnp.dot(weights[:, PAGE:], pool_ref[1, 1], preferred_element_type=F32)
    for r in range(decodes):
        span = slice(r * HEADS, (r + 1) * HEADS)
        mixed = dec_scores[span, :] + own[span, :] * new_values[r : r + 1, :]
        dec_context[r : r + 1, :] = jnp.sum(
            jnp.where(mine, mixed, 0.0), axis=0, keepdims=True
        )
    for c in range(chunks):
        dec_wide[:, c, :] = dec_context[:, c * LANES : (c + 1) * LANES]
    dec_rows[...] = dec_wide[...].astype(BF16)
    first.wait()
    turn = lax.div(head[0, 0], even_rows)
    for p in range(near):
        j = lax.rem(p + 2 * devices - turn - decodes * lax.rem(me, 2), near)
        near_send[p] = dec_rows[jnp.minimum(j, decodes - 1)]

    _, _, page = cached_positions(0, (PAGE, width), 0)
    first_page = page == 0
    keys[0:PAGE, :] = jnp.where(
        first_page, pool_ref[0, 0].astype(F32), pool_ref[1, 0].astype(F32)
    ).astype(BF16)
    values[0:PAGE, :] = jnp.where(
        first_page, pool_ref[0, 1].astype(F32), pool_ref[1, 1].astype(F32)
    ).astype(BF16)
    extended[6:8, :] = state[0]
    extended[8 : 8 + rows, :] = qkv_ref[1].astype(F32)
    keys[PAGE : PAGE + rows, :] = (
        taps_ref[0:1, :] * extended[6 : 6 + rows, :]
        + taps_ref[1:2, :] * extended[7 : 7 + rows, :]
        + taps_ref[2:3, :] * extended[8 : 8 + rows, :]
    ).astype(BF16)
    values[PAGE : PAGE + rows, :] = qkv_ref[2]

    cached, position, _ = cached_positions(0, (rows, PAGE), 1)
    token = iota((rows, PAGE), 0)
    ok_cached = (position >= 0) & (position >= cached + token - (WINDOW - 1))
    other = iota((rows, rows), 1)
    token = iota((rows, rows), 0)
    ok_fresh = (other <= token) & (other >= token - (WINDOW - 1))
    bias = jnp.concatenate(
        [
            jnp.where(ok_cached, 0.0, masked_score).astype(F32),
            jnp.where(ok_fresh, 0.0, masked_score).astype(F32),
        ],
        axis=1,
    )
    context[...] = jnp.zeros_like(context)

    def attend(head):
        low, high = head * HEAD_CHANNELS, (head + 1) * HEAD_CHANNELS
        start = low // LANES * LANES
        stop = -(-high // LANES) * LANES
        lane = iota((rows, stop - start), 1) + start
        mine = (lane >= low) & (lane < high)
        query = jnp.where(mine, qkv_ref[0, :, start:stop].astype(F32), 0.0).astype(BF16)
        scores = dot_nt(query, keys[:, start:stop]) * scale + bias
        top = jnp.max(scores, axis=1, keepdims=True)
        raised = jnp.exp(scores - top)
        weights = (raised * (1.0 / jnp.sum(raised, axis=1, keepdims=True))).astype(BF16)
        part = jnp.dot(weights, values[:, start:stop], preferred_element_type=F32)
        context[:, start:stop] = jnp.where(mine, part, context[:, start:stop])

    for head in range(HEADS // 2):
        attend(head)

    pl.semaphore_wait(barrier, devices - 1)

    near_recv[place] = near_send[place]

    @pl.loop(1, near)
    def _(step):
        goal = lax.rem(place + step, near)
        pltpu.make_async_remote_copy(
            src_ref=near_send.at[goal],
            dst_ref=near_recv.at[place],
            send_sem=near_sems.at[0],
            recv_sem=near_sems.at[1],
            device_id={"req": plane * near + goal},
            device_id_type=MESH,
        ).start()

    for head in range(HEADS // 2, HEADS):
        attend(head)

    def drain(ref, count, sem):
        span = ref.at[pl.ds(0, count)]
        pltpu.make_async_copy(span, span, sem).wait()

    drain(near_recv, near - 1, near_sems.at[1])
    for p in range(far):
        u = lax.rem(p * near + place + devices - turn, devices)
        far_send[p] = near_recv[lax.div(u, decodes)]

    @pl.loop(1, far)
    def _(step):
        goal = lax.rem(plane + step, far)
        pltpu.make_async_remote_copy(
            src_ref=far_send.at[goal],
            dst_ref=arrived_ref.at[devices + plane],
            send_sem=far_sems.at[0],
            recv_sem=far_sems.at[1],
            device_id={"req": goal * near + place},
            device_id_type=MESH,
        ).start()

    order = iota((devices, rows), 0) * STRIDE + me - turn
    chosen = (order & (devices - 1)) == iota((devices, rows), 1)
    context[...] = jnp.dot(
        chosen.astype(F32).astype(BF16),
        context[...].astype(BF16),
        preferred_element_type=F32,
    )
    for c in range(chunks):
        wide[:, c, :] = context[:, c * LANES : (c + 1) * LANES]
    send[...] = wide[...].astype(BF16)

    @pl.loop(1, devices)
    def _(step):
        pltpu.make_async_remote_copy(
            src_ref=send.at[step],
            dst_ref=arrived_ref.at[me],
            send_sem=send_sem,
            recv_sem=recv_sem,
            device_id={"req": lax.rem(me + step * STRIDE, devices)},
            device_id_type=MESH,
        ).start()

    kept = pltpu.make_async_copy(send.at[0], arrived_ref.at[me], own_sems.at[0])
    kept.start()
    kept_far = pltpu.make_async_copy(
        far_send.at[plane], arrived_ref.at[devices + plane], own_sems.at[1]
    )
    kept_far.start()
    kept.wait()
    kept_far.wait()
    drain(near_send, near - 1, near_sems.at[0])
    drain(far_send, far - 1, far_sems.at[0])
    drain(arrived_ref, far - 1, far_sems.at[1])
    drain(send, devices - 1, send_sem)
    drain(arrived_ref, devices - 1, recv_sem)


def finish_kernel(
    devices,
    arrived_ref,
    residual_ref,
    gain_ref,
    regroup_ref,
    owner_ref,
    sum_ref,
    norm_ref,
    wide,
    rows,
):
    me = lax.axis_index("req")
    even_rows, width = residual_ref.shape
    decodes = even_rows - devices
    token = (me - rotation(regroup_ref, even_rows, devices)) & (devices - 1)

    column = jnp.sum(
        jnp.where(iota((even_rows, devices), 1) == token, regroup_ref[...], 0),
        axis=1,
        keepdims=True,
    ) - me * even_rows

    def lands(part):
        size = part.shape[0]
        diagonal = iota((size, size), 0) == iota((size, size), 1)
        row = jnp.sum(jnp.where(diagonal, part, 0), axis=0, keepdims=True)
        return (iota((even_rows, size), 0) == row).astype(F32).astype(BF16)

    diagonal = iota((devices, devices), 0) == iota((devices, devices), 1)
    owner = jnp.sum(jnp.where(diagonal, owner_ref[...], 0), axis=1, keepdims=True)
    came = (iota((devices, devices), 1) == owner).astype(F32).astype(BF16)
    pick = jnp.dot(lands(column[:devices]), came, preferred_element_type=F32).astype(BF16)
    wide[...] = arrived_ref[...].astype(F32)
    for c in range(width // LANES):
        rows[:, c * LANES : (c + 1) * LANES] = wide[:, c, :].astype(BF16)
    gathered = jnp.dot(pick, rows[:devices, :], preferred_element_type=F32)
    gathered += jnp.dot(
        lands(column[devices:]), rows[devices:, :], preferred_element_type=F32
    )
    summed = residual_ref[...].astype(F32) + gathered
    inverse_rms = lax.rsqrt(jnp.mean(summed * summed, axis=1, keepdims=True) + norm_eps)
    sum_ref[...] = summed.astype(BF16)
    norm_ref[...] = (summed * inverse_rms * gain_ref[...]).astype(BF16)


def body(
    prefill_qkv,
    decode_qkv,
    conv_state,
    cache_len,
    page_table,
    page_pool,
    conv_taps,
    segment_owner,
    regroup,
    residual,
    norm_gain,
):
    devices = lax.axis_size("req")
    rows, _, width = prefill_qkv.shape
    decodes = decode_qkv.shape[0]
    even_rows = residual.shape[0]
    chunks = width // LANES
    near = devices // decodes
    table = regroup.reshape(regroup.shape[0] // devices, devices)
    owner = segment_owner.reshape(1, devices)
    smem = pl.BlockSpec(memory_space=pltpu.SMEM)
    vmem = pl.BlockSpec(memory_space=pltpu.VMEM)
    hbm = pl.BlockSpec(memory_space=pl.ANY)
    arrived = pl.pallas_call(
        functools.partial(exchange_kernel, devices, even_rows),
        out_shape=jax.ShapeDtypeStruct((even_rows, chunks, LANES), BF16),
        in_specs=[smem, smem, hbm] + [vmem] * 5,
        out_specs=hbm,
        scratch_shapes=[
            pltpu.VMEM((rows + 8, width), F32),
            pltpu.VMEM((PAGE + rows, width), BF16),
            pltpu.VMEM((PAGE + rows, width), BF16),
            pltpu.VMEM((rows, width), F32),
            pltpu.VMEM((decodes * HEADS, width), BF16),
            pltpu.VMEM((decodes * HEADS, width), F32),
            pltpu.VMEM(conv_state.shape, F32),
            pltpu.VMEM((decodes, width), F32),
            pltpu.VMEM((devices, chunks, LANES), F32),
            pltpu.VMEM((decodes, chunks, LANES), F32),
            pltpu.VMEM((devices, chunks, LANES), BF16),
            pltpu.VMEM((decodes, chunks, LANES), BF16),
            pltpu.VMEM((near, chunks, LANES), BF16),
            pltpu.VMEM((near, chunks, LANES), BF16),
            pltpu.VMEM((decodes, chunks, LANES), BF16),
            pltpu.SemaphoreType.DMA,
            pltpu.SemaphoreType.DMA,
            pltpu.SemaphoreType.DMA((2,)),
            pltpu.SemaphoreType.DMA((2,)),
            pltpu.SemaphoreType.DMA((2,)),
            pltpu.SMEM((8, devices), I32),
        ],
        compiler_params=pltpu.CompilerParams(collective_id=0, has_side_effects=True),
        name="exchange",
    )(
        cache_len,
        page_table,
        table,
        prefill_qkv.transpose(1, 0, 2),
        decode_qkv.transpose(1, 0, 2),
        conv_state,
        page_pool,
        conv_taps,
    )
    out = jax.ShapeDtypeStruct((even_rows, width), BF16)
    return pl.pallas_call(
        functools.partial(finish_kernel, devices),
        out_shape=(out, out),
        in_specs=[vmem] * 5,
        out_specs=(vmem, vmem),
        scratch_shapes=[
            pltpu.VMEM((even_rows, chunks, LANES), F32),
            pltpu.VMEM((even_rows, width), BF16),
        ],
        name="finish",
    )(arrived, residual, norm_gain.reshape(1, width), table, owner)


def solution(mesh):
    in_specs = (
        P(("rep", "req"), None, None),
        P(("rep", "req"), None, None),
        P(("rep", "req"), None, None),
        P(("rep", "req")),
        P(("rep", "req"), None),
        P(("rep", "req"), None, None, None),
        P(),
        P("rep"),
        P("rep"),
        P(("rep", "req"), None),
        P(),
    )
    out_specs = (P(("rep", "req"), None), P(("rep", "req"), None))
    return jax.shard_map(body, mesh=mesh, in_specs=in_specs, out_specs=out_specs, check_vma=False)
```

time: 72.9 us -> 46.7 us (0.64)
  Pallas kernels: 13 us -> 44.5 us
  waiting for transfers between devices: 28 us -> 0 us
  starting transfers between devices: 18.4 us -> 0 us
  local copies, waits for them, and re-layouts: 10 us -> 1.3 us
  other arithmetic: 2.48 us -> 0 us
    pallas_call x1, Pallas kernels: 9.77 us -> 40.7 us  [body(): pl.pallas_call(functools.partial(exchange_kernel, devices, even_rows), ou...]
    all_to_all x1 -> x0, waiting for transfers between devices: 28 us -> none  [body(): lax.all_to_all(packed, 'req', split_axis=0, concat_axis=0, tiled=True)]
    all_to_all x1 -> x0, starting transfers between devices: 18.4 us -> none  [body(): lax.all_to_all(packed, 'req', split_axis=0, concat_axis=0, tiled=True)]
    squeeze x4 -> x0, local copies, waits for them, and re-layouts: 4.96 us -> none  [the longest x1 2.4 us: body(): prefill_qkv[:, 2]]
    unnamed x7 -> x0, local copies, waits for them, and re-layouts: 2.94 us -> none
    all_to_all x1 -> x0, other arithmetic: 2.48 us -> none  [body(): lax.all_to_all(packed, 'req', split_axis=0, concat_axis=0, tiled=True)]
    slice x1 -> x0, local copies, waits for them, and re-layouts: 1 us -> none  [body(): conv_state[1:, 1]]
  transfers between devices with their start and end apart: 1 -> 0, of which waited for: 1 -> 0; matrix products, arithmetic and copies ran while one was open for 1% -> 0% of each run, Pallas kernels for 0% -> 0%
where the time goes in v1:
time: 46.7 us; the launch traced here: 46.4 us
  Pallas kernels  44.5 us (95%)
  local copies, waits for them, and re-layouts  1.3 us (3%)
  between operations  0.64 us (1%)
    pallas_call x1, Pallas kernels, body(): pl.pallas_call(functools.partial(exchange_kernel, devices, even_rows), ou...  40.7 us
    pallas_call x1, Pallas kernels, body(): pl.pallas_call(functools.partial(finish_kernel, devices), out_shape=(out,...  3.77 us
    reshape x1, local copies, waits for them, and re-layouts, body(): norm_gain.reshape(1, width)  1.3 us

profile of v1, /device:TPU:1, one launch (start us, length us, event | category | flops | bytes accessed | tf_op | source)
XLA Modules:
  0.0 46.4 jit_solution(17098544967455431212)
XLA Ops:
  0.6 1.3 %reshape.14.gain_ref = f32[1,1792]{1,0:T(1,128)} reshape(f32[1792]{0:T(1024)} %param.21) | data formatting | bytes 14336 | tf_op jit(solution)/shard_map/reshape | solution.py:411
  1.9 40.7 %exchange.1.arrived_ref = bf16[136,14,128]{2,1,0:T(8,128)(2,1)} custom-call(s32[9]{0:T(128)} %cache_len_ref.1, s32[9,256]{1,0:T(8,128)} %page_table_ref.1, s32[136,128]{1,0:T(8,128)} %bitcast.5, bf16[3,128,1792]{2,1,0:T(8,128)(2,1)} %bitcast.4, bf16[3,8,1792]{2,1,0:T(8,128)(2,1)} %bitcast.7, bf16[9,2,1792]{2,1,0:T(2,128)(2,1)} %state_ref.1, ...), custom_call_target="tpu_custom_call" | custom-call | tf_op jit(solution)/shard_map/exchange/pallas_call | solution.py:360
  42.6 3.8 %finish.1 = (bf16[136,1792]{1,0:T(8,128)(2,1)}, bf16[136,1792]{1,0:T(8,128)(2,1)}) custom-call(bf16[136,14,128]{2,1,0:T(8,128)(2,1)} %exchange.1.arrived_ref, bf16[136,1792]{1,0:T(8,128)(2,1)} %residual_ref.1, f32[1,1792]{1,0:T(1,128)} %reshape.14.gain_ref, s32[136,128]{1,0:T(8,128)} %bitcast.6, s32[1,128]{1,0:T(1,128)} %bitcast.8), custom_call_target="tpu_custom_call" | custom-call | tf_op jit(solution)/shard_map/finish/pallas_call | solution.py:401

commit v2 on v1

--- a/solution.py
+++ b/solution.py
@@ -12,7 +12,6 @@
 WINDOW = 64
 PAGE = 128
 LANES = 128
-STRIDE = 37
 MESH = pl.DeviceIdType.MESH
 
 norm_eps = 1e-06
@@ -34,6 +33,10 @@
     first = regroup_ref[0:1, 0:1]
     starts = iota((1, devices), 1) * even_rows
     return jnp.sum((starts <= first).astype(I32), axis=1, keepdims=True) - 1
+
+
+def offset_of(rank):
+    return 4 + ((rank + 1) // 2) * (1 - 2 * (rank % 2))
 
 
 def exchange_kernel(
@@ -48,6 +51,7 @@
     pool_ref,
     taps_ref,
     arrived_ref,
+    far_ref,
     extended,
     keys,
     values,
@@ -63,8 +67,8 @@
     near_send,
     near_recv,
     far_send,
-    send_sem,
-    recv_sem,
+    send_sems,
+    recv_sems,
     near_sems,
     far_sems,
     own_sems,
@@ -78,6 +82,8 @@
     near = devices // decodes
     far = decodes
     place, plane = lax.rem(me, near), lax.div(me, near)
+    column, core = lax.div(place, 2), lax.rem(place, 2)
+    half = width // 2
     scale = HEAD_CHANNELS ** (-0.5)
     first = pltpu.make_async_copy(
         table_ref.at[pl.ds(0, 8)], head, own_sems.at[0]
@@ -104,6 +110,124 @@
         return cached, position, page
 
     state[...] = state_ref[...].astype(F32)
+
+    first.wait()
+    turn = lax.div(head[0, 0], even_rows)
+    _, _, page = cached_positions(0, (PAGE, width), 0)
+    first_page = page == 0
+    keys[0:PAGE, :] = jnp.where(
+        first_page, pool_ref[0, 0].astype(F32), pool_ref[1, 0].astype(F32)
+    ).astype(BF16)
+    values[0:PAGE, :] = jnp.where(
+        first_page, pool_ref[0, 1].astype(F32), pool_ref[1, 1].astype(F32)
+    ).astype(BF16)
+    extended[6:8, :] = state[0]
+    extended[8 : 8 + rows, :] = qkv_ref[1].astype(F32)
+    keys[PAGE : PAGE + rows, :] = (
+        taps_ref[0:1, :] * extended[6 : 6 + rows, :]
+        + taps_ref[1:2, :] * extended[7 : 7 + rows, :]
+        + taps_ref[2:3, :] * extended[8 : 8 + rows, :]
+    ).astype(BF16)
+    values[PAGE : PAGE + rows, :] = qkv_ref[2]
+
+    def fresh_bias(begin, count):
+        other = iota((WINDOW, count), 1)
+        token = iota((WINDOW, count), 0) + begin
+        ok = (other <= token) & (other >= token - (WINDOW - 1))
+        return jnp.where(ok, 0.0, masked_score).astype(F32)
+
+    cached, position, _ = cached_positions(0, (WINDOW, PAGE), 1)
+    token = iota((WINDOW, PAGE), 0)
+    ok = (position >= 0) & (position >= cached + token - (WINDOW - 1))
+    bands = [
+        (
+            0,
+            0,
+            PAGE + WINDOW,
+            jnp.concatenate(
+                [jnp.where(ok, 0.0, masked_score).astype(F32), fresh_bias(0, WINDOW)],
+                axis=1,
+            ),
+        )
+    ]
+    for begin in range(WINDOW, rows, WINDOW):
+        first_key = begin - WINDOW
+        bands.append((begin, PAGE + first_key, 2 * WINDOW, fresh_bias(WINDOW, 2 * WINDOW)))
+    context[...] = jnp.zeros_like(context)
+
+    def attend(head):
+        low, high = head * HEAD_CHANNELS, (head + 1) * HEAD_CHANNELS
+        start = low // LANES * LANES
+        stop = -(-high // LANES) * LANES
+        lane = iota((WINDOW, stop - start), 1) + start
+        mine = (lane >= low) & (lane < high)
+        for begin, key, count, bias in bands:
+            block = slice(begin, begin + WINDOW)
+            query = qkv_ref[0, block, start:stop].astype(F32)
+            query = jnp.where(mine, query, 0.0).astype(BF16)
+            scores = dot_nt(query, keys[key : key + count, start:stop]) * scale + bias
+            top = jnp.max(scores, axis=1, keepdims=True)
+            raised = jnp.exp(scores - top)
+            share = 1.0 / jnp.sum(raised, axis=1, keepdims=True)
+            part = jnp.dot(
+                (raised * share).astype(BF16),
+                values[key : key + count, start:stop],
+                preferred_element_type=F32,
+            )
+            context[block, start:stop] = jnp.where(mine, part, context[block, start:stop])
+
+    slot = iota((devices, rows), 0)
+
+    def offsets(rank):
+        return 4 + ((rank + 1) >> 1) * (1 - 2 * (rank & 1))
+
+    target = (
+        ((plane + offsets(slot >> 4)) & (far - 1)) * near
+        + ((column + offsets((slot >> 1) & 7)) & 7) * 2
+        + ((core + 1 + slot) & 1)
+    )
+    chosen = ((target - turn) & (devices - 1)) == iota((devices, rows), 1)
+    chosen = chosen.astype(F32).astype(BF16)
+
+    def send_half(side):
+        span = slice(side * half, (side + 1) * half)
+        context[:, span] = jnp.dot(
+            chosen, context[:, span].astype(BF16), preferred_element_type=F32
+        )
+        for c in range(chunks // 2):
+            low = side * half + c * LANES
+            wide[:, c, :] = context[:, low : low + LANES]
+        send[side] = wide[...].astype(BF16)
+
+        def to_chip(rank_z, rank_y, cores):
+            goal_z = lax.rem(plane + offset_of(rank_z), far)
+            goal_y = lax.rem(column + offset_of(rank_y), 8)
+            for c in range(cores):
+                goal_core = lax.rem(core + 1 + c, 2)
+                pltpu.make_async_remote_copy(
+                    src_ref=send.at[side, (rank_z * 8 + rank_y) * 2 + c],
+                    dst_ref=arrived_ref.at[side, me],
+                    send_sem=send_sems.at[side],
+                    recv_sem=recv_sems.at[side],
+                    device_id={"req": goal_z * near + goal_y * 2 + goal_core},
+                    device_id_type=MESH,
+                ).start()
+
+        for shell in range(far):
+            if shell:
+
+                @pl.loop(0, shell)
+                def _(rank):
+                    to_chip(shell, rank, 2)
+                    to_chip(rank, shell, 2)
+
+            to_chip(shell, shell, 2 if shell < far - 1 else 1)
+
+    for head in range(HEADS // 2):
+        attend(head)
+
+    pl.semaphore_wait(barrier, devices - 1)
+    send_half(0)
 
     lane = iota((HEADS, width), 1)
     low = iota((HEADS, width), 0) * HEAD_CHANNELS
@@ -155,62 +279,9 @@
     for c in range(chunks):
         dec_wide[:, c, :] = dec_context[:, c * LANES : (c + 1) * LANES]
     dec_rows[...] = dec_wide[...].astype(BF16)
-    first.wait()
-    turn = lax.div(head[0, 0], even_rows)
     for p in range(near):
         j = lax.rem(p + 2 * devices - turn - decodes * lax.rem(me, 2), near)
         near_send[p] = dec_rows[jnp.minimum(j, decodes - 1)]
-
-    _, _, page = cached_positions(0, (PAGE, width), 0)
-    first_page = page == 0
-    keys[0:PAGE, :] = jnp.where(
-        first_page, pool_ref[0, 0].astype(F32), pool_ref[1, 0].astype(F32)
-    ).astype(BF16)
-    values[0:PAGE, :] = jnp.where(
-        first_page, pool_ref[0, 1].astype(F32), pool_ref[1, 1].astype(F32)
-    ).astype(BF16)
-    extended[6:8, :] = state[0]
-    extended[8 : 8 + rows, :] = qkv_ref[1].astype(F32)
-    keys[PAGE : PAGE + rows, :] = (
-        taps_ref[0:1, :] * extended[6 : 6 + rows, :]
-        + taps_ref[1:2, :] * extended[7 : 7 + rows, :]
-        + taps_ref[2:3, :] * extended[8 : 8 + rows, :]
-    ).astype(BF16)
-    values[PAGE : PAGE + rows, :] = qkv_ref[2]
-
-    cached, position, _ = cached_positions(0, (rows, PAGE), 1)
-    token = iota((rows, PAGE), 0)
-    ok_cached = (position >= 0) & (position >= cached + token - (WINDOW - 1))
-    other = iota((rows, rows), 1)
-    token = iota((rows, rows), 0)
-    ok_fresh = (other <= token) & (other >= token - (WINDOW - 1))
-    bias = jnp.concatenate(
-        [
-            jnp.where(ok_cached, 0.0, masked_score).astype(F32),
-            jnp.where(ok_fresh, 0.0, masked_score).astype(F32),
-        ],
-        axis=1,
-    )
-    context[...] = jnp.zeros_like(context)
-
-    def attend(head):
-        low, high = head * HEAD_CHANNELS, (head + 1) * HEAD_CHANNELS
-        start = low // LANES * LANES
-        stop = -(-high // LANES) * LANES
-        lane = iota((rows, stop - start), 1) + start
-        mine = (lane >= low) & (lane < high)
-        query = jnp.where(mine, qkv_ref[0, :, start:stop].astype(F32), 0.0).astype(BF16)
-        scores = dot_nt(query, keys[:, start:stop]) * scale + bias
-        top = jnp.max(scores, axis=1, keepdims=True)
-        raised = jnp.exp(scores - top)
-        weights = (raised * (1.0 / jnp.sum(raised, axis=1, keepdims=True))).astype(BF16)
-        part = jnp.dot(weights, values[:, start:stop], preferred_element_type=F32)
-        context[:, start:stop] = jnp.where(mine, part, context[:, start:stop])
-
-    for head in range(HEADS // 2):
-        attend(head)
-
-    pl.semaphore_wait(barrier, devices - 1)
 
     near_recv[place] = near_send[place]
 
@@ -228,6 +299,7 @@
 
     for head in range(HEADS // 2, HEADS):
         attend(head)
+    send_half(1)
 
     def drain(ref, count, sem):
         span = ref.at[pl.ds(0, count)]
@@ -243,53 +315,38 @@
         goal = lax.rem(plane + step, far)
         pltpu.make_async_remote_copy(
             src_ref=far_send.at[goal],
-            dst_ref=arrived_ref.at[devices + plane],
+            dst_ref=far_ref.at[plane],
             send_sem=far_sems.at[0],
             recv_sem=far_sems.at[1],
             device_id={"req": goal * near + place},
             device_id_type=MESH,
         ).start()
 
-    order = iota((devices, rows), 0) * STRIDE + me - turn
-    chosen = (order & (devices - 1)) == iota((devices, rows), 1)
-    context[...] = jnp.dot(
-        chosen.astype(F32).astype(BF16),
-        context[...].astype(BF16),
-        preferred_element_type=F32,
-    )
-    for c in range(chunks):
-        wide[:, c, :] = context[:, c * LANES : (c + 1) * LANES]
-    send[...] = wide[...].astype(BF16)
-
-    @pl.loop(1, devices)
-    def _(step):
-        pltpu.make_async_remote_copy(
-            src_ref=send.at[step],
-            dst_ref=arrived_ref.at[me],
-            send_sem=send_sem,
-            recv_sem=recv_sem,
-            device_id={"req": lax.rem(me + step * STRIDE, devices)},
-            device_id_type=MESH,
-        ).start()
-
-    kept = pltpu.make_async_copy(send.at[0], arrived_ref.at[me], own_sems.at[0])
-    kept.start()
-    kept_far = pltpu.make_async_copy(
-        far_send.at[plane], arrived_ref.at[devices + plane], own_sems.at[1]
-    )
-    kept_far.start()
-    kept.wait()
-    kept_far.wait()
+    kept = [
+        pltpu.make_async_copy(
+            send.at[side, devices - 1], arrived_ref.at[side, me], own_sems.at[side]
+        )
+        for side in range(2)
+    ]
+    kept.append(
+        pltpu.make_async_copy(far_send.at[plane], far_ref.at[plane], own_sems.at[2])
+    )
+    for copy in kept:
+        copy.start()
+    for copy in kept:
+        copy.wait()
     drain(near_send, near - 1, near_sems.at[0])
     drain(far_send, far - 1, far_sems.at[0])
-    drain(arrived_ref, far - 1, far_sems.at[1])
-    drain(send, devices - 1, send_sem)
-    drain(arrived_ref, devices - 1, recv_sem)
+    drain(far_ref, far - 1, far_sems.at[1])
+    for side in range(2):
+        drain(send.at[side], devices - 1, send_sems.at[side])
+        drain(arrived_ref.at[side], devices - 1, recv_sems.at[side])
 
 
 def finish_kernel(
     devices,
     arrived_ref,
+    far_ref,
     residual_ref,
     gain_ref,
     regroup_ref,
@@ -297,6 +354,7 @@
     sum_ref,
     norm_ref,
     wide,
+    far_wide,
     rows,
 ):
     me = lax.axis_index("req")
@@ -321,8 +379,12 @@
     came = (iota((devices, devices), 1) == owner).astype(F32).astype(BF16)
     pick = jnp.dot(lands(column[:devices]), came, preferred_element_type=F32).astype(BF16)
     wide[...] = arrived_ref[...].astype(F32)
+    far_wide[...] = far_ref[...].astype(F32)
+    half = wide.shape[2]
     for c in range(width // LANES):
-        rows[:, c * LANES : (c + 1) * LANES] = wide[:, c, :].astype(BF16)
+        span = slice(c * LANES, (c + 1) * LANES)
+        rows[:devices, span] = wide[c // half, :, c % half, :].astype(BF16)
+        rows[devices:, span] = far_wide[:, c, :].astype(BF16)
     gathered = jnp.dot(pick, rows[:devices, :], preferred_element_type=F32)
     gathered += jnp.dot(
         lands(column[devices:]), rows[devices:, :], preferred_element_type=F32
@@ -330,7 +392,7 @@
     summed = residual_ref[...].astype(F32) + gathered
     inverse_rms = lax.rsqrt(jnp.mean(summed * summed, axis=1, keepdims=True) + norm_eps)
     sum_ref[...] = summed.astype(BF16)
-    norm_ref[...] = (summed * inverse_rms * gain_ref[...]).astype(BF16)
+    norm_ref[...] = (summed * inverse_rms * gain_ref[...].reshape(1, width)).astype(BF16)
 
 
 def body(
@@ -357,11 +419,14 @@
     smem = pl.BlockSpec(memory_space=pltpu.SMEM)
     vmem = pl.BlockSpec(memory_space=pltpu.VMEM)
     hbm = pl.BlockSpec(memory_space=pl.ANY)
-    arrived = pl.pallas_call(
+    arrived, far = pl.pallas_call(
         functools.partial(exchange_kernel, devices, even_rows),
-        out_shape=jax.ShapeDtypeStruct((even_rows, chunks, LANES), BF16),
+        out_shape=(
+            jax.ShapeDtypeStruct((2, devices, chunks // 2, LANES), BF16),
+            jax.ShapeDtypeStruct((decodes, chunks, LANES), BF16),
+        ),
         in_specs=[smem, smem, hbm] + [vmem] * 5,
-        out_specs=hbm,
+        out_specs=(hbm, hbm),
         scratch_shapes=[
             pltpu.VMEM((rows + 8, width), F32),
             pltpu.VMEM((PAGE + rows, width), BF16),
@@ -371,18 +436,18 @@
             pltpu.VMEM((decodes * HEADS, width), F32),
             pltpu.VMEM(conv_state.shape, F32),
             pltpu.VMEM((decodes, width), F32),
-            pltpu.VMEM((devices, chunks, LANES), F32),
+            pltpu.VMEM((devices, chunks // 2, LANES), F32),
             pltpu.VMEM((decodes, chunks, LANES), F32),
-            pltpu.VMEM((devices, chunks, LANES), BF16),
+            pltpu.VMEM((2, devices, chunks // 2, LANES), BF16),
             pltpu.VMEM((decodes, chunks, LANES), BF16),
             pltpu.VMEM((near, chunks, LANES), BF16),
             pltpu.VMEM((near, chunks, LANES), BF16),
             pltpu.VMEM((decodes, chunks, LANES), BF16),
-            pltpu.SemaphoreType.DMA,
-            pltpu.SemaphoreType.DMA,
             pltpu.SemaphoreType.DMA((2,)),
             pltpu.SemaphoreType.DMA((2,)),
             pltpu.SemaphoreType.DMA((2,)),
+            pltpu.SemaphoreType.DMA((2,)),
+            pltpu.SemaphoreType.DMA((3,)),
             pltpu.SMEM((8, devices), I32),
         ],
         compiler_params=pltpu.CompilerParams(collective_id=0, has_side_effects=True),
@@ -401,14 +466,15 @@
     return pl.pallas_call(
         functools.partial(finish_kernel, devices),
         out_shape=(out, out),
-        in_specs=[vmem] * 5,
+        in_specs=[vmem] * 6,
         out_specs=(vmem, vmem),
         scratch_shapes=[
-            pltpu.VMEM((even_rows, chunks, LANES), F32),
+            pltpu.VMEM((2, devices, chunks // 2, LANES), F32),
+            pltpu.VMEM((decodes, chunks, LANES), F32),
             pltpu.VMEM((even_rows, width), BF16),
         ],
         name="finish",
-    )(arrived, residual, norm_gain.reshape(1, width), table, owner)
+    )(arrived, far, residual, norm_gain, table, owner)
 
 
 def solution(mesh):

time: 46.7 us -> 41.7 us (0.89)
  Pallas kernels: 44.5 us -> 40.9 us
  local copies, waits for them, and re-layouts: 1.3 us -> 0 us
    pallas_call x1, Pallas kernels: 40.7 us -> 37.1 us  [body(): pl.pallas_call(functools.partial(exchange_kernel, devices, even_rows), ou...]
    reshape x1 -> x0, local copies, waits for them, and re-layouts: 1.3 us -> none  [body(): norm_gain.reshape(1, width)]
where the time goes in v2:
time: 41.7 us; the launch traced here: 41.5 us
  Pallas kernels  40.9 us (98%)
  between operations  0.64 us (2%)
    pallas_call x1, Pallas kernels, body(): pl.pallas_call(functools.partial(exchange_kernel, devices, even_rows), ou...  37.1 us
    pallas_call x1, Pallas kernels, body(): pl.pallas_call(functools.partial(finish_kernel, devices), out_shape=(out,...  3.74 us

profile of v2, /device:TPU:1, one launch (start us, length us, event | category | flops | bytes accessed | tf_op | source)
XLA Modules:
  0.0 41.5 jit_solution(522544557225587213)
XLA Ops:
  0.6 37.1 %exchange.1 = (bf16[2,128,7,128]{3,2,1,0:T(8,128)(2,1)}, bf16[8,14,128]{2,1,0:T(8,128)(2,1)}) custom-call(s32[9]{0:T(128)} %cache_len_ref.1, s32[9,256]{1,0:T(8,128)} %page_table_ref.1, s32[136,128]{1,0:T(8,128)} %bitcast.5, bf16[3,128,1792]{2,1,0:T(8,128)(2,1)} %bitcast.4, bf16[3,8,1792]{2,1,0:T(8,128)(2,1)} %bitcast.7, bf16[9,2,1792]{2,1,0:T(2,128)(2,1)} %state_ref.1, ...), custom_call_target="tpu_custom_call" | custom-call | tf_op jit(solution)/shard_map/exchange/pallas_call | solution.py:422
  37.8 3.7 %finish.1 = (bf16[136,1792]{1,0:T(8,128)(2,1)}, bf16[136,1792]{1,0:T(8,128)(2,1)}) custom-call(bf16[2,128,7,128]{3,2,1,0:T(8,128)(2,1)} %get-tuple-element.4.arrived_ref, bf16[8,14,128]{2,1,0:T(8,128)(2,1)} %get-tuple-element.5.far_ref, bf16[136,1792]{1,0:T(8,128)(2,1)} %residual_ref.1, f32[1792]{0:T(1024)} %gain_ref.1, s32[136,128]{1,0:T(8,128)} %bitcast.6, ...), custom_call_target="tpu_custom_call" | custom-call | tf_op jit(solution)/shard_map/finish/pallas_call | solution.py:466

commit v3 on v2

v3 whole, which is shorter than its diff:
```python
import functools

import jax
import jax.numpy as jnp
from jax import lax
from jax.experimental import pallas as pl
from jax.experimental.pallas import tpu as pltpu
from jax.sharding import PartitionSpec as P

HEADS = 16
HEAD_CHANNELS = 112
WINDOW = 64
PAGE = 128
LANES = 128
EARLY_LANES = 1024
EARLY_HEADS = -(-EARLY_LANES // HEAD_CHANNELS)
MESH = pl.DeviceIdType.MESH

norm_eps = 1e-06
masked_score = -1e30
F32 = jnp.float32
BF16 = jnp.bfloat16
I32 = jnp.int32


def iota(shape, dim):
    return lax.broadcasted_iota(I32, shape, dim)


def dot_nt(a, b):
    return lax.dot_general(a, b, (((1,), (1,)), ((), ())), preferred_element_type=F32)


def offset_of(rank):
    return 4 + ((rank + 1) // 2) * (1 - 2 * (rank % 2))


def exchange_kernel(
    devices,
    even_rows,
    cache_len_ref,
    page_table_ref,
    table_ref,
    qkv_ref,
    dqkv_ref,
    state_ref,
    pool_ref,
    taps_ref,
    regroup_ref,
    owner_ref,
    gathered_ref,
    extended,
    keys,
    values,
    context,
    dec_queries,
    dec_scores,
    state,
    dec_context,
    wide,
    dec_wide,
    send_0,
    send_1,
    recv_0,
    recv_1,
    far_recv,
    dec_rows,
    near_send,
    near_recv,
    far_send,
    send_sems,
    recv_sems,
    near_sems,
    far_sems,
    own_sems,
    head,
):
    me = lax.axis_index("req")
    rows = qkv_ref.shape[1]
    width = qkv_ref.shape[2]
    decodes = dqkv_ref.shape[1]
    chunks = width // LANES
    near = devices // decodes
    far = decodes
    place, plane = lax.rem(me, near), lax.div(me, near)
    column, core = lax.div(place, 2), lax.rem(place, 2)
    spans = [slice(0, EARLY_LANES), slice(EARLY_LANES, width)]
    scale = HEAD_CHANNELS ** (-0.5)
    first = pltpu.make_async_copy(
        table_ref.at[pl.ds(0, 8)], head, own_sems.at[0]
    )
    first.start()

    send, recv = (send_0, send_1), (recv_0, recv_1)
    barrier = pltpu.get_barrier_semaphore()

    @pl.loop(1, devices)
    def _(step):
        peer = lax.rem(me + step, devices)
        pl.semaphore_signal(
            barrier, inc=1, device_id={"req": peer}, device_id_type=MESH
        )

    def cached_positions(r, shape, dim):
        cached = cache_len_ref[r]
        top = jnp.maximum((cached - 1) >> 7, 0)
        below = jnp.maximum(top - 1, 0)
        at_top, at_below = page_table_ref[r, top], page_table_ref[r, below]
        offset = iota(shape, dim)
        position = cached - 1 - ((cached - 1 - offset) & (PAGE - 1))
        page = jnp.where(position >= top * PAGE, at_top, at_below)
        return cached, position, page

    state[...] = state_ref[...].astype(F32)

    first.wait()
    turn = lax.div(head[0, 0], even_rows)
    lane = iota((HEADS, width), 1)
    low = iota((HEADS, width), 0) * HEAD_CHANNELS
    mine = (lane >= low) & (lane < low + HEAD_CHANNELS)
    fresh = (
        taps_ref[0:1, :] * state[1 : 1 + decodes, 0, :]
        + taps_ref[1:2, :] * state[1 : 1 + decodes, 1, :]
        + taps_ref[2:3, :] * dqkv_ref[1].astype(F32)
    ).astype(BF16).astype(F32)
    queries = dqkv_ref[0].astype(F32)
    new_values = dqkv_ref[2].astype(F32)
    own = []
    bias_rows = []
    for r in range(decodes):
        spread = jnp.where(mine, queries[r : r + 1, :], 0.0)
        dec_queries[r * HEADS : (r + 1) * HEADS, :] = spread.astype(BF16)
        own.append(jnp.sum(spread * fresh[r : r + 1, :], axis=1, keepdims=True))
        cached, position, page = cached_positions(1 + r, (HEADS, PAGE), 1)
        ok = (position >= 0) & (position >= cached - (WINDOW - 1))
        bias_rows.append(
            jnp.concatenate(
                [
                    jnp.where(ok & (page == n), 0.0, masked_score).astype(F32)
                    for n in range(2)
                ],
                axis=1,
            )
        )
    own = jnp.concatenate(own, axis=0) * scale
    scores = jnp.concatenate(
        [dot_nt(dec_queries[...], pool_ref[n, 0]) for n in range(2)], axis=1
    )
    scores = scores * scale + jnp.concatenate(bias_rows, axis=0)
    top = jnp.maximum(jnp.max(scores, axis=1, keepdims=True), own)
    raised = jnp.exp(scores - top)
    own = jnp.exp(own - top)
    total = 1.0 / (jnp.sum(raised, axis=1, keepdims=True) + own)
    weights = (raised * total).astype(BF16)
    own = (own * total).astype(BF16).astype(F32)
    dec_scores[...] = jnp.dot(
        weights[:, :PAGE], pool_ref[0, 1], preferred_element_type=F32
    ) + jnp.dot(weights[:, PAGE:], pool_ref[1, 1], preferred_element_type=F32)
    for r in range(decodes):
        span = slice(r * HEADS, (r + 1) * HEADS)
        mixed = dec_scores[span, :] + own[span, :] * new_values[r : r + 1, :]
        dec_context[r : r + 1, :] = jnp.sum(
            jnp.where(mine, mixed, 0.0), axis=0, keepdims=True
        )
    for c in range(chunks):
        dec_wide[:, c, :] = dec_context[:, c * LANES : (c + 1) * LANES]
    dec_rows[...] = dec_wide[...].astype(BF16)
    for p in range(near):
        j = lax.rem(p + 2 * devices - turn - decodes * lax.rem(me, 2), near)
        near_send[p] = dec_rows[jnp.minimum(j, decodes - 1)]

    _, _, page = cached_positions(0, (PAGE, width), 0)
    first_page = page == 0
    keys[0:PAGE, :] = jnp.where(
        first_page, pool_ref[0, 0].astype(F32), pool_ref[1, 0].astype(F32)
    ).astype(BF16)
    values[0:PAGE, :] = jnp.where(
        first_page, pool_ref[0, 1].astype(F32), pool_ref[1, 1].astype(F32)
    ).astype(BF16)
    extended[6:8, :] = state[0]
    extended[8 : 8 + rows, :] = qkv_ref[1].astype(F32)
    keys[PAGE : PAGE + rows, :] = (
        taps_ref[0:1, :] * extended[6 : 6 + rows, :]
        + taps_ref[1:2, :] * extended[7 : 7 + rows, :]
        + taps_ref[2:3, :] * extended[8 : 8 + rows, :]
    ).astype(BF16)
    values[PAGE : PAGE + rows, :] = qkv_ref[2]

    def fresh_bias(begin, count):
        other = iota((WINDOW, count), 1)
        token = iota((WINDOW, count), 0) + begin
        ok = (other <= token) & (other >= token - (WINDOW - 1))
        return jnp.where(ok, 0.0, masked_score).astype(F32)

    cached, position, _ = cached_positions(0, (WINDOW, PAGE), 1)
    token = iota((WINDOW, PAGE), 0)
    ok = (position >= 0) & (position >= cached + token - (WINDOW - 1))
    bands = [
        (
            0,
            0,
            PAGE + WINDOW,
            jnp.concatenate(
                [jnp.where(ok, 0.0, masked_score).astype(F32), fresh_bias(0, WINDOW)],
                axis=1,
            ),
        )
    ]
    for begin in range(WINDOW, rows, WINDOW):
        first_key = begin - WINDOW
        bands.append((begin, PAGE + first_key, 2 * WINDOW, fresh_bias(WINDOW, 2 * WINDOW)))
    context[...] = jnp.zeros_like(context)

    def attend(head):
        low, high = head * HEAD_CHANNELS, (head + 1) * HEAD_CHANNELS
        start = low // LANES * LANES
        stop = -(-high // LANES) * LANES
        lane = iota((WINDOW, stop - start), 1) + start
        mine = (lane >= low) & (lane < high)
        for begin, key, count, bias in bands:
            block = slice(begin, begin + WINDOW)
            query = qkv_ref[0, block, start:stop].astype(F32)
            query = jnp.where(mine, query, 0.0).astype(BF16)
            scores = dot_nt(query, keys[key : key + count, start:stop]) * scale + bias
            top = jnp.max(scores, axis=1, keepdims=True)
            raised = jnp.exp(scores - top)
            share = 1.0 / jnp.sum(raised, axis=1, keepdims=True)
            part = jnp.dot(
                (raised * share).astype(BF16),
                values[key : key + count, start:stop],
                preferred_element_type=F32,
            )
            context[block, start:stop] = jnp.where(mine, part, context[block, start:stop])

    slot = iota((devices, rows), 0)

    def offsets(rank):
        return 4 + ((rank + 1) >> 1) * (1 - 2 * (rank & 1))

    target = (
        ((plane + offsets(slot >> 4)) & (far - 1)) * near
        + ((column + offsets((slot >> 1) & 7)) & 7) * 2
        + ((core + 1 + slot) & 1)
    )
    chosen = ((target - turn) & (devices - 1)) == iota((devices, rows), 1)
    chosen = chosen.astype(F32).astype(BF16)

    def send_half(side):
        span = spans[side]
        sent = jnp.dot(
            chosen, context[:, span].astype(BF16), preferred_element_type=F32
        )
        count = (span.stop - span.start) // LANES
        for c in range(count):
            wide[:, c, :] = sent[:, c * LANES : (c + 1) * LANES]
        send[side][...] = wide[:, :count, :].astype(BF16)

        def to_chip(rank_z, rank_y, cores):
            goal_z = lax.rem(plane + offset_of(rank_z), far)
            goal_y = lax.rem(column + offset_of(rank_y), 8)
            for c in range(cores):
                goal_core = lax.rem(core + 1 + c, 2)
                pltpu.make_async_remote_copy(
                    src_ref=send[side].at[(rank_z * 8 + rank_y) * 2 + c],
                    dst_ref=recv[side].at[me],
                    send_sem=send_sems.at[side],
                    recv_sem=recv_sems.at[side],
                    device_id={"req": goal_z * near + goal_y * 2 + goal_core},
                    device_id_type=MESH,
                ).start()

        for shell in range(far):
            if shell:

                @pl.loop(0, shell)
                def _(rank):
                    to_chip(shell, rank, 2)
                    to_chip(rank, shell, 2)

            to_chip(shell, shell, 2 if shell < far - 1 else 1)

    for head in range(EARLY_HEADS):
        attend(head)

    pl.semaphore_wait(barrier, devices - 1)

    near_recv[place] = near_send[place]

    @pl.loop(1, near)
    def _(step):
        goal = lax.rem(place + step, near)
        pltpu.make_async_remote_copy(
            src_ref=near_send.at[goal],
            dst_ref=near_recv.at[place],
            send_sem=near_sems.at[0],
            recv_sem=near_sems.at[1],
            device_id={"req": plane * near + goal},
            device_id_type=MESH,
        ).start()

    send_half(0)
    for head in range(EARLY_HEADS, HEADS):
        attend(head)

    def drain(ref, count, sem):
        span = ref.at[pl.ds(0, count)]
        pltpu.make_async_copy(span, span, sem).wait()

    drain(near_recv, near - 1, near_sems.at[1])
    for p in range(far):
        u = lax.rem(p * near + place + devices - turn, devices)
        far_send[p] = near_recv[lax.div(u, decodes)]

    @pl.loop(1, far)
    def _(step):
        goal = lax.rem(plane + step, far)
        pltpu.make_async_remote_copy(
            src_ref=far_send.at[goal],
            dst_ref=far_recv.at[plane],
            send_sem=far_sems.at[0],
            recv_sem=far_sems.at[1],
            device_id={"req": goal * near + place},
            device_id_type=MESH,
        ).start()

    send_half(1)

    kept = [
        pltpu.make_async_copy(
            send[side].at[devices - 1], recv[side].at[me], own_sems.at[side]
        )
        for side in range(2)
    ]
    kept.append(
        pltpu.make_async_copy(far_send.at[plane], far_recv.at[plane], own_sems.at[2])
    )
    for copy in kept:
        copy.start()
    for copy in kept:
        copy.wait()
    drain(near_send, near - 1, near_sems.at[0])
    drain(far_send, far - 1, far_sems.at[0])
    for side in range(2):
        drain(send[side], devices - 1, send_sems.at[side])

    token = lax.rem(me + devices - turn, devices)
    landing = jnp.sum(
        jnp.where(iota((even_rows, devices), 1) == token, regroup_ref[...], 0),
        axis=1,
        keepdims=True,
    ) - me * even_rows

    def lands(part):
        size = part.shape[0]
        diagonal = iota((size, size), 0) == iota((size, size), 1)
        row = jnp.sum(jnp.where(diagonal, part, 0), axis=0, keepdims=True)
        return (iota((even_rows, size), 0) == row).astype(F32).astype(BF16)

    diagonal = iota((devices, devices), 0) == iota((devices, devices), 1)
    owner = jnp.sum(jnp.where(diagonal, owner_ref[...], 0), axis=1, keepdims=True)
    came = (iota((devices, devices), 1) == owner).astype(F32).astype(BF16)
    pick = jnp.dot(
        lands(landing[:devices]), came, preferred_element_type=F32
    ).astype(BF16)
    pick_far = lands(landing[devices:])

    drain(far_recv, far - 1, far_sems.at[1])
    dec_wide[...] = far_recv[...].astype(F32)
    for c in range(chunks):
        dec_context[:, c * LANES : (c + 1) * LANES] = dec_wide[:, c, :]
    far_rows = jnp.dot(
        pick_far, dec_context[...].astype(BF16), preferred_element_type=F32
    )
    for side in range(2):
        span = spans[side]
        count = (span.stop - span.start) // LANES
        drain(recv[side], devices - 1, recv_sems.at[side])
        wide[:, :count, :] = recv[side][...].astype(F32)
        for c in range(count):
            low = span.start + c * LANES
            row = wide[:, c, :].astype(BF16)
            gathered_ref[:, low : low + LANES] = (
                jnp.dot(pick, row, preferred_element_type=F32)
                + far_rows[:, low : low + LANES]
            ).astype(BF16)


def finish_kernel(gathered_ref, residual_ref, gain_ref, sum_ref, norm_ref):
    width = residual_ref.shape[1]
    summed = residual_ref[...].astype(F32) + gathered_ref[...].astype(F32)
    inverse_rms = lax.rsqrt(jnp.mean(summed * summed, axis=1, keepdims=True) + norm_eps)
    sum_ref[...] = summed.astype(BF16)
    norm_ref[...] = (summed * inverse_rms * gain_ref[...].reshape(1, width)).astype(BF16)


def body(
    prefill_qkv,
    decode_qkv,
    conv_state,
    cache_len,
    page_table,
    page_pool,
    conv_taps,
    segment_owner,
    regroup,
    residual,
    norm_gain,
):
    devices = lax.axis_size("req")
    rows, _, width = prefill_qkv.shape
    decodes = decode_qkv.shape[0]
    even_rows = residual.shape[0]
    chunks = width // LANES
    near = devices // decodes
    table = regroup.reshape(regroup.shape[0] // devices, devices)
    owner = segment_owner.reshape(1, devices)
    smem = pl.BlockSpec(memory_space=pltpu.SMEM)
    vmem = pl.BlockSpec(memory_space=pltpu.VMEM)
    early = EARLY_LANES // LANES
    out = jax.ShapeDtypeStruct((even_rows, width), BF16)
    hbm = pl.BlockSpec(memory_space=pl.ANY)
    gathered = pl.pallas_call(
        functools.partial(exchange_kernel, devices, even_rows),
        out_shape=out,
        in_specs=[smem, smem, hbm] + [vmem] * 7,
        out_specs=vmem,
        scratch_shapes=[
            pltpu.VMEM((rows + 8, width), F32),
            pltpu.VMEM((PAGE + rows, width), BF16),
            pltpu.VMEM((PAGE + rows, width), BF16),
            pltpu.VMEM((rows, width), F32),
            pltpu.VMEM((decodes * HEADS, width), BF16),
            pltpu.VMEM((decodes * HEADS, width), F32),
            pltpu.VMEM(conv_state.shape, F32),
            pltpu.VMEM((decodes, width), F32),
            pltpu.VMEM((devices, early, LANES), F32),
            pltpu.VMEM((decodes, chunks, LANES), F32),
            pltpu.VMEM((devices, early, LANES), BF16),
            pltpu.VMEM((devices, chunks - early, LANES), BF16),
            pltpu.VMEM((devices, early, LANES), BF16),
            pltpu.VMEM((devices, chunks - early, LANES), BF16),
            pltpu.VMEM((decodes, chunks, LANES), BF16),
            pltpu.VMEM((decodes, chunks, LANES), BF16),
            pltpu.VMEM((near, chunks, LANES), BF16),
            pltpu.VMEM((near, chunks, LANES), BF16),
            pltpu.VMEM((decodes, chunks, LANES), BF16),
            pltpu.SemaphoreType.DMA((2,)),
            pltpu.SemaphoreType.DMA((2,)),
            pltpu.SemaphoreType.DMA((2,)),
            pltpu.SemaphoreType.DMA((2,)),
            pltpu.SemaphoreType.DMA((3,)),
            pltpu.SMEM((8, devices), I32),
        ],
        compiler_params=pltpu.CompilerParams(collective_id=0, has_side_effects=True),
        name="exchange",
    )(
        cache_len,
        page_table,
        table,
        prefill_qkv.transpose(1, 0, 2),
        decode_qkv.transpose(1, 0, 2),
        conv_state,
        page_pool,
        conv_taps,
        table,
        owner,
    )
    return pl.pallas_call(
        finish_kernel,
        out_shape=(out, out),
        in_specs=[vmem] * 3,
        out_specs=(vmem, vmem),
        name="finish",
    )(gathered, residual, norm_gain)


def solution(mesh):
    in_specs = (
        P(("rep", "req"), None, None),
        P(("rep", "req"), None, None),
        P(("rep", "req"), None, None),
        P(("rep", "req")),
        P(("rep", "req"), None),
        P(("rep", "req"), None, None, None),
        P(),
        P("rep"),
        P("rep"),
        P(("rep", "req"), None),
        P(),
    )
    out_specs = (P(("rep", "req"), None), P(("rep", "req"), None))
    return jax.shard_map(body, mesh=mesh, in_specs=in_specs, out_specs=out_specs, check_vma=False)
```

time: 41.7 us -> 41.7 us (level)
    pallas_call x1, Pallas kernels: 37.1 us -> 38.6 us  [body(): pl.pallas_call(functools.partial(exchange_kernel, devices, even_rows), ou...]
    pallas_call x1, Pallas kernels: 3.74 us -> 2.34 us  [body(): pl.pallas_call(finish_kernel, out_shape=(out, out), in_specs=[vmem] * 3,...]
where the time goes in v3:
time: 41.7 us; the launch traced here: 41.6 us
  Pallas kernels  40.9 us (98%)
  between operations  0.64 us (2%)
    pallas_call x1, Pallas kernels, body(): pl.pallas_call(functools.partial(exchange_kernel, devices, even_rows), ou...  38.6 us
    pallas_call x1, Pallas kernels, body(): pl.pallas_call(finish_kernel, out_shape=(out, out), in_specs=[vmem] * 3,...  2.34 us

profile of v3, /device:TPU:1, one launch (start us, length us, event | category | flops | bytes accessed | tf_op | source)
XLA Modules:
  0.0 41.6 jit_solution(4234149123740313193)
XLA Ops:
  0.6 38.6 %exchange.1.gathered_ref = bf16[136,1792]{1,0:T(8,128)(2,1)} custom-call(s32[9]{0:T(128)} %cache_len_ref.1, s32[9,256]{1,0:T(8,128)} %page_table_ref.1, s32[136,128]{1,0:T(8,128)} %bitcast.5, bf16[3,128,1792]{2,1,0:T(8,128)(2,1)} %bitcast.4, bf16[3,8,1792]{2,1,0:T(8,128)(2,1)} %bitcast.7, bf16[9,2,1792]{2,1,0:T(2,128)(2,1)} %state_ref.1, ...), custom_call_target="tpu_custom_call" | custom-call | tf_op jit(solution)/shard_map/exchange/pallas_call | solution.py:422
  39.2 2.3 %finish.1 = (bf16[136,1792]{1,0:T(8,128)(2,1)}, bf16[136,1792]{1,0:T(8,128)(2,1)}) custom-call(bf16[136,1792]{1,0:T(8,128)(2,1)} %exchange.1.gathered_ref, bf16[136,1792]{1,0:T(8,128)(2,1)} %residual_ref.1, f32[1792]{0:T(1024)} %gain_ref.1), custom_call_target="tpu_custom_call" | custom-call | tf_op jit(solution)/shard_map/finish/pallas_call | solution.py:468

commit v4 on v3

--- a/solution.py
+++ b/solution.py
@@ -41,13 +41,13 @@
     cache_len_ref,
     page_table_ref,
     table_ref,
-    qkv_ref,
-    dqkv_ref,
-    state_ref,
-    pool_ref,
-    taps_ref,
-    regroup_ref,
-    owner_ref,
+    qkv_hbm,
+    dqkv_hbm,
+    state_hbm,
+    pool_hbm,
+    taps_hbm,
+    regroup_hbm,
+    owner_hbm,
     gathered_ref,
     extended,
     keys,
@@ -74,6 +74,14 @@
     far_sems,
     own_sems,
     head,
+    qkv_ref,
+    dqkv_ref,
+    state_ref,
+    pool_ref,
+    taps_ref,
+    regroup_ref,
+    owner_ref,
+    load_sems,
 ):
     me = lax.axis_index("req")
     rows = qkv_ref.shape[1]
@@ -90,16 +98,36 @@
         table_ref.at[pl.ds(0, 8)], head, own_sems.at[0]
     )
     first.start()
+    loads = [
+        pltpu.make_async_copy(source, target, load_sems.at[n])
+        for n, (source, target) in enumerate(
+            [
+                (dqkv_hbm, dqkv_ref),
+                (state_hbm, state_ref),
+                (taps_hbm, taps_ref),
+                (pool_hbm, pool_ref),
+                (qkv_hbm, qkv_ref),
+                (regroup_hbm, regroup_ref),
+                (owner_hbm, owner_ref),
+            ]
+        )
+    ]
+    for load in loads:
+        load.start()
 
     send, recv = (send_0, send_1), (recv_0, recv_1)
     barrier = pltpu.get_barrier_semaphore()
 
-    @pl.loop(1, devices)
-    def _(step):
-        peer = lax.rem(me + step, devices)
+    def greet(step):
         pl.semaphore_signal(
-            barrier, inc=1, device_id={"req": peer}, device_id_type=MESH
-        )
+            barrier,
+            inc=1,
+            device_id={"req": lax.rem(me + step, devices)},
+            device_id_type=MESH,
+        )
+
+    pl.loop(devices // 2, devices)(greet)
+    pl.loop(1, devices // 2)(greet)
 
     def cached_positions(r, shape, dim):
         cached = cache_len_ref[r]
@@ -111,6 +139,8 @@
         page = jnp.where(position >= top * PAGE, at_top, at_below)
         return cached, position, page
 
+    for load in loads[:4]:
+        load.wait()
     state[...] = state_ref[...].astype(F32)
 
     first.wait()
@@ -169,6 +199,7 @@
         j = lax.rem(p + 2 * devices - turn - decodes * lax.rem(me, 2), near)
         near_send[p] = dec_rows[jnp.minimum(j, decodes - 1)]
 
+    loads[4].wait()
     _, _, page = cached_positions(0, (PAGE, width), 0)
     first_page = page == 0
     keys[0:PAGE, :] = jnp.where(
@@ -270,13 +301,9 @@
                 ).start()
 
         for shell in range(far):
-            if shell:
-
-                @pl.loop(0, shell)
-                def _(rank):
-                    to_chip(shell, rank, 2)
-                    to_chip(rank, shell, 2)
-
+            for rank in range(shell):
+                to_chip(shell, rank, 2)
+                to_chip(rank, shell, 2)
             to_chip(shell, shell, 2 if shell < far - 1 else 1)
 
     for head in range(EARLY_HEADS):
@@ -343,6 +370,8 @@
     for side in range(2):
         drain(send[side], devices - 1, send_sems.at[side])
 
+    loads[5].wait()
+    loads[6].wait()
     token = lax.rem(me + devices - turn, devices)
     landing = jnp.sum(
         jnp.where(iota((even_rows, devices), 1) == token, regroup_ref[...], 0),
@@ -422,7 +451,7 @@
     gathered = pl.pallas_call(
         functools.partial(exchange_kernel, devices, even_rows),
         out_shape=out,
-        in_specs=[smem, smem, hbm] + [vmem] * 7,
+        in_specs=[smem, smem] + [hbm] * 8,
         out_specs=vmem,
         scratch_shapes=[
             pltpu.VMEM((rows + 8, width), F32),
@@ -450,6 +479,14 @@
             pltpu.SemaphoreType.DMA((2,)),
             pltpu.SemaphoreType.DMA((3,)),
             pltpu.SMEM((8, devices), I32),
+            pltpu.VMEM((3, rows, width), BF16),
+            pltpu.VMEM((3, decodes, width), BF16),
+            pltpu.VMEM(conv_state.shape, BF16),
+            pltpu.VMEM(page_pool.shape, BF16),
+            pltpu.VMEM(conv_taps.shape, F32),
+            pltpu.VMEM(table.shape, I32),
+            pltpu.VMEM(owner.shape, I32),
+            pltpu.SemaphoreType.DMA((7,)),
         ],
         compiler_params=pltpu.CompilerParams(collective_id=0, has_side_effects=True),
         name="exchange",

time: 41.7 us -> 41.4 us (level)
  no operation moved by 1% of the time
where the time goes in v4:
time: 41.4 us; the launch traced here: 41.2 us
  Pallas kernels  40.5 us (98%)
  between operations  0.64 us (2%)
    pallas_call x1, Pallas kernels, body(): pl.pallas_call(functools.partial(exchange_kernel, devices, even_rows), ou...  38.2 us
    pallas_call x1, Pallas kernels, body(): pl.pallas_call(finish_kernel, out_shape=(out, out), in_specs=[vmem] * 3,...  2.34 us

profile of v4, /device:TPU:1, one launch (start us, length us, event | category | flops | bytes accessed | tf_op | source)
XLA Modules:
  0.0 41.2 jit_solution(4530477631635309278)
XLA Ops:
  0.6 38.2 %exchange.1.gathered_ref = bf16[136,1792]{1,0:T(8,128)(2,1)} custom-call(s32[9]{0:T(128)} %cache_len_ref.1, s32[9,256]{1,0:T(8,128)} %page_table_ref.1, s32[136,128]{1,0:T(8,128)} %bitcast.5, bf16[3,128,1792]{2,1,0:T(8,128)(2,1)} %bitcast.4, bf16[3,8,1792]{2,1,0:T(8,128)(2,1)} %bitcast.7, bf16[9,2,1792]{2,1,0:T(2,128)(2,1)} %state_hbm.1, ...), custom_call_target="tpu_custom_call" | custom-call | tf_op jit(solution)/shard_map/exchange/pallas_call | solution.py:451
  38.8 2.3 %finish.1 = (bf16[136,1792]{1,0:T(8,128)(2,1)}, bf16[136,1792]{1,0:T(8,128)(2,1)}) custom-call(bf16[136,1792]{1,0:T(8,128)(2,1)} %exchange.1.gathered_ref, bf16[136,1792]{1,0:T(8,128)(2,1)} %residual_ref.1, f32[1792]{0:T(1024)} %gain_ref.1), custom_call_target="tpu_custom_call" | custom-call | tf_op jit(solution)/shard_map/finish/pallas_call | solution.py:505

commit v5 on v4

--- a/solution.py
+++ b/solution.py
@@ -31,8 +31,17 @@
     return lax.dot_general(a, b, (((1,), (1,)), ((), ())), preferred_element_type=F32)
 
 
-def offset_of(rank):
-    return 4 + ((rank + 1) // 2) * (1 - 2 * (rank % 2))
+def chip_offsets(side):
+    reach = side // 2
+    pairs = [(a, b) for a in range(reach + 1) for b in range(reach + 1)]
+    pairs.sort(key=lambda pair: (-sum(pair), pair))
+    steps = []
+    for a, b in pairs:
+        for step in ((a, b), (-a, -b), (a, -b), (-a, b)):
+            step = (step[0] % side, step[1] % side)
+            if step not in steps:
+                steps.append(step)
+    return steps
 
 
 def exchange_kernel(
@@ -265,12 +274,10 @@
 
     slot = iota((devices, rows), 0)
 
-    def offsets(rank):
-        return 4 + ((rank + 1) >> 1) * (1 - 2 * (rank & 1))
-
+    turning = 1 - 2 * core
     target = (
-        ((plane + offsets(slot >> 4)) & (far - 1)) * near
-        + ((column + offsets((slot >> 1) & 7)) & 7) * 2
+        ((plane + far + turning * (slot >> 4)) & (far - 1)) * near
+        + ((column + far + turning * ((slot >> 1) & 7)) & 7) * 2
         + ((core + 1 + slot) & 1)
     )
     chosen = ((target - turn) & (devices - 1)) == iota((devices, rows), 1)
@@ -286,25 +293,19 @@
             wide[:, c, :] = sent[:, c * LANES : (c + 1) * LANES]
         send[side][...] = wide[:, :count, :].astype(BF16)
 
-        def to_chip(rank_z, rank_y, cores):
-            goal_z = lax.rem(plane + offset_of(rank_z), far)
-            goal_y = lax.rem(column + offset_of(rank_y), 8)
-            for c in range(cores):
+        for step_z, step_y in chip_offsets(far):
+            goal_z = lax.rem(plane + far + turning * step_z, far)
+            goal_y = lax.rem(column + far + turning * step_y, far)
+            for c in range(2 if step_z or step_y else 1):
                 goal_core = lax.rem(core + 1 + c, 2)
                 pltpu.make_async_remote_copy(
-                    src_ref=send[side].at[(rank_z * 8 + rank_y) * 2 + c],
+                    src_ref=send[side].at[(step_z * far + step_y) * 2 + c],
                     dst_ref=recv[side].at[me],
                     send_sem=send_sems.at[side],
                     recv_sem=recv_sems.at[side],
                     device_id={"req": goal_z * near + goal_y * 2 + goal_core},
                     device_id_type=MESH,
                 ).start()
-
-        for shell in range(far):
-            for rank in range(shell):
-                to_chip(shell, rank, 2)
-                to_chip(rank, shell, 2)
-            to_chip(shell, shell, 2 if shell < far - 1 else 1)
 
     for head in range(EARLY_HEADS):
         attend(head)
@@ -354,7 +355,7 @@
 
     kept = [
         pltpu.make_async_copy(
-            send[side].at[devices - 1], recv[side].at[me], own_sems.at[side]
+            send[side].at[1], recv[side].at[me], own_sems.at[side]
         )
         for side in range(2)
     ]

time: 41.4 us -> 41.1 us (level)
  no operation moved by 1% of the time
where the time goes in v5:
time: 41.1 us; the launch traced here: 40.8 us
  Pallas kernels  40.2 us (98%)
  between operations  0.64 us (2%)
    pallas_call x1, Pallas kernels, body(): pl.pallas_call(functools.partial(exchange_kernel, devices, even_rows), ou...  37.9 us
    pallas_call x1, Pallas kernels, body(): pl.pallas_call(finish_kernel, out_shape=(out, out), in_specs=[vmem] * 3,...  2.34 us

profile of v5, /device:TPU:1, one launch (start us, length us, event | category | flops | bytes accessed | tf_op | source)
XLA Modules:
  0.0 40.8 jit_solution(17079574330772875021)
XLA Ops:
  0.6 37.9 %exchange.1.gathered_ref = bf16[136,1792]{1,0:T(8,128)(2,1)} custom-call(s32[9]{0:T(128)} %cache_len_ref.1, s32[9,256]{1,0:T(8,128)} %page_table_ref.1, s32[136,128]{1,0:T(8,128)} %bitcast.5, bf16[3,128,1792]{2,1,0:T(8,128)(2,1)} %bitcast.4, bf16[3,8,1792]{2,1,0:T(8,128)(2,1)} %bitcast.7, bf16[9,2,1792]{2,1,0:T(2,128)(2,1)} %state_hbm.1, ...), custom_call_target="tpu_custom_call" | custom-call | tf_op jit(solution)/shard_map/exchange/pallas_call | solution.py:452
  38.5 2.3 %finish.1 = (bf16[136,1792]{1,0:T(8,128)(2,1)}, bf16[136,1792]{1,0:T(8,128)(2,1)}) custom-call(bf16[136,1792]{1,0:T(8,128)(2,1)} %exchange.1.gathered_ref, bf16[136,1792]{1,0:T(8,128)(2,1)} %residual_ref.1, f32[1792]{0:T(1024)} %gain_ref.1), custom_call_target="tpu_custom_call" | custom-call | tf_op jit(solution)/shard_map/finish/pallas_call | solution.py:506
